TPU v7x, 32 devices: a whole 2x2x4 slice. The times are simulated.
32 devices in a mesh: slab: 8 (over y, x, core), grp: 4 (over z).
Axes of the slice: x: 2, y: 2, z: 4, core: 2. Of those that a mesh axis runs over, the one named last changes fastest.
Arguments:
- near_field: bfloat16 [2, 4096, 2048], P(None, 'slab', 'grp'), may hold values from -6 to 6
- lens_phase: float32 [2, 4096, 2048], P(None, 'slab', 'grp'), may hold values from -3.140625 to 3.140625
Outputs:
- far_field: float32 [2, 512, 2048], P(None, ('slab', 'grp'))
All inputs are finite; a program needn't handle non-finite values.
Results may differ from a plain program's by a relative error of at most 0.0083.
Values may be sent and summed in bfloat16 or wider, within the bound.
A program may use at most 128 MiB of HBM per device.

v0:
```python
import math
import jax
import jax.numpy as jnp
from jax import lax
from jax.sharding import PartitionSpec as P

AV = 512
AL = 2048
PHASE_CODE = 40.0


def sincos(angle):
    half = 0.5 * angle
    sq = half * half
    sin = -1.0 / 39916800.0
    for term in (1.0 / 362880.0, -1.0 / 5040.0, 1.0 / 120.0, -1.0 / 6.0, 1.0):
        sin = sin * sq + term
    sin = sin * half
    cos = 1.0 / 479001600.0
    for term in (-1.0 / 3628800.0, 1.0 / 40320.0, -1.0 / 720.0, 1.0 / 24.0, -0.5, 1.0):
        cos = cos * sq + term
    return (1.0 - 2.0 * sin * sin, 2.0 * sin * cos)


def unit_angle(turns, modulus):
    assert modulus & modulus - 1 == 0
    centred = (turns + modulus // 2 & modulus - 1) - modulus // 2
    return sincos(centred.astype(jnp.float32) * (2.0 * math.pi / modulus))


def count(size):
    return lax.optimization_barrier(jnp.arange(size, dtype=jnp.int32))


def phase_table(row_index, col_index, modulus):
    cos, sin = unit_angle(row_index[:, None] * col_index[None, :], modulus)
    return (cos.astype(jnp.bfloat16), sin.astype(jnp.bfloat16))


def propagator(points):
    band = math.gcd(points, 128)
    offset = count(points)[None, :] - count(band)[:, None]
    cos, sin = unit_angle(offset * offset - points // 4, 2 * points)
    gain = 1.0 / math.sqrt(points)

    def rolled(part):
        part = lax.optimization_barrier((part * gain).astype(jnp.bfloat16))
        twice = jnp.concatenate([part, part], axis=1)
        return jnp.concatenate(
            [
                lax.slice_in_dim(twice, points - start, 2 * points - start, axis=1)
                for start in range(0, points, band)
            ]
        )

    return (rolled(cos), rolled(sin))


def matmul(left, right):
    return jnp.dot(left, right, preferred_element_type=jnp.float32)


def complex_product(both, table_cos, table_sin):
    rows = both.shape[0] // 2
    with_cos = matmul(both, table_cos)
    with_sin = matmul(both, table_sin)
    return (with_cos[:rows] - with_sin[rows:], with_sin[:rows] + with_cos[rows:])


def on_device(near_field, lens_phase):
    slab_count = lax.axis_size("slab")
    group_count = lax.axis_size("grp")
    devices = slab_count * group_count
    steps, lat_dev, width = lens_phase.shape
    points = width * group_count
    total_rows = lat_dev * slab_count
    rows = lat_dev // group_count
    angles = AV // devices
    coded = [jnp.exp2(lens_phase[k] * PHASE_CODE).astype(jnp.bfloat16) for k in range(steps)]
    field = lax.all_to_all(near_field, "grp", split_axis=1, concat_axis=2, tiled=True)
    coded = [lax.all_to_all(part, "grp", split_axis=0, concat_axis=1, tiled=True) for part in coded]
    prop_cos, prop_sin = propagator(points)
    both = field.reshape(2 * rows, points)
    for section in range(steps):
        real, imag = complex_product(both, prop_cos, prop_sin)
        real = real.astype(jnp.bfloat16).astype(jnp.float32)
        imag = imag.astype(jnp.bfloat16).astype(jnp.float32)
        phase = jnp.log2(coded[section].astype(jnp.float32)) * (1.0 / PHASE_CODE)
        lens_cos, lens_sin = sincos(phase)
        both = jnp.concatenate(
            [
                (real * lens_cos - imag * lens_sin).astype(jnp.bfloat16),
                (real * lens_sin + imag * lens_cos).astype(jnp.bfloat16),
            ]
        )
    vert_cos, vert_sin = phase_table(count(points) - points // 2, count(AV) - AV // 2, 2 * points)
    col_real, col_imag = complex_product(both, vert_cos, -vert_sin)
    cols = jnp.stack([col_real, col_imag]).astype(jnp.bfloat16)
    cols = jnp.transpose(cols.reshape(2, rows, devices, angles), (2, 0, 3, 1))
    got = lax.all_to_all(cols, ("slab", "grp"), split_axis=0, concat_axis=0, tiled=True)
    modulus = 2 * total_rows
    period = modulus // rows
    source = count(devices) - devices // 2
    fine = count(period)
    near = count(rows)
    coarse = count(AL // period)
    w_cos, w_sin = phase_table(source, fine, period)
    got_real = got[:, 0]
    got_imag = got[:, 1]
    ein = lambda s, l, r: jnp.einsum(s, l, r, preferred_element_type=jnp.float32)
    mid_real = ein("sam,sf->afm", got_real, w_cos) + ein("sam,sf->afm", got_imag, w_sin)
    mid_imag = ein("sam,sf->afm", got_imag, w_cos) - ein("sam,sf->afm", got_real, w_sin)
    t_cos, t_sin = unit_angle(fine[:, None] * near[None, :], modulus)
    turned_real = (mid_real * t_cos + mid_imag * t_sin).astype(jnp.bfloat16)
    turned_imag = (mid_imag * t_cos - mid_real * t_sin).astype(jnp.bfloat16)
    e_cos, e_sin = phase_table(near, coarse * period - AL // 2, modulus)
    out_real = ein("afm,mc->acf", turned_real, e_cos) + ein("afm,mc->acf", turned_imag, e_sin)
    out_imag = ein("afm,mc->acf", turned_imag, e_cos) - ein("afm,mc->acf", turned_real, e_sin)
    scale = 1.0 / math.sqrt(total_rows * points)
    return (jnp.stack([out_real, out_imag]) * scale).reshape(2, angles, AL)


def solution(mesh):
    return jax.shard_map(
        on_device,
        mesh=mesh,
        in_specs=(P(None, "slab", "grp"), P(None, "slab", "grp")),
        out_specs=P(None, ("slab", "grp"), None),
        check_vma=False,
    )
```

profile of v0, /device:TPU:0, one launch (start us, length us, event | category | flops | bytes accessed | tf_op | source)
XLA Modules:
  0.0 123.4 jit_solution(17463661891979874556)
XLA Ops:
  0.0 2.8 %exponential_convert_fusion.1 = (bf16[1,512,512]{2,1,0:T(8,128)(2,1)}, bf16[1,512,512]{2,1,0:T(8,128)(2,1)}) fusion(f32[2,512,512]{2,1,0:T(8,128)} %param.3), kind=kLoop, calls=%fused_computation.138 | loop fusion | flops 1048576 | bytes 3145728 | tf_op jit(solution)/shard_map/convert_element_type | solution.py:79
  2.8 6.3 %all-to-all-start.1 = ((bf16[4,128,512]{2,1,0:T(8,128)(2,1)}), bf16[4,128,512]{2,1,0:T(8,128)(2,1)S(1)}, u32[]{:S(2)}, u32[]{:S(2)}) async-start(bf16[4,128,512]{2,1,0:T(8,128)(2,1)} %bitcast.6), calls=%async_computation.1 | async-start | bytes 1048576 | tf_op jit(solution)/shard_map/all_to_all | solution.py:81
  9.2 1.4 %fusion.27 = (bf16[128,2048]{1,0:T(8,128)(2,1)S(1)}, bf16[128,2048]{1,0:T(8,128)(2,1)S(1)}) fusion(s32[128]{0:T(128)S(1)} %iota.18, s32[2048]{0:T(1024)S(1)} %iota.21), kind=kLoop, calls=%fused_computation.108 | loop fusion | flops 10223616 | bytes 1057280 | tf_op jit(solution)/shard_map/convert_element_type | solution.py:47
  11.3 0.0 copy-start.2
  11.3 0.9 constant_dynamic-update-slice_fusion
  12.2 1.3 %fusion.76 = bf16[2048,2048]{1,0:T(8,128)(2,1)} fusion(bf16[2048,2048]{1,0:T(8,128)(2,1)} %constant_dynamic-update-slice_fusion, bf16[128,2048]{1,0:T(8,128)(2,1)S(1)} %get-tuple-element.20), kind=kLoop, calls=%fused_computation.180 | loop fusion | flops 1048576 | bytes 1048576
  13.6 0.8 fusion.78
  14.4 0.9 fusion.80
  15.3 0.8 fusion.82
  16.1 0.8 fusion.84
  16.9 0.8 fusion.86
  17.8 0.9 fusion.88
  18.6 0.0 copy-done.2
  18.6 0.9 fusion.90
  19.5 4.1 %all-to-all-done.1 = bf16[4,128,512]{2,1,0:T(8,128)(2,1)S(1)} async-done(((bf16[4,128,512]{2,1,0:T(8,128)(2,1)}), bf16[4,128,512]{2,1,0:T(8,128)(2,1)S(1)}, u32[]{:S(2)}, u32[]{:S(2)}) %all-to-all-start.1) | async-done | bytes 524320 | tf_op jit(solution)/shard_map/all_to_all | solution.py:81
  23.6 3.5 %all-to-all-start.2 = ((bf16[4,128,512]{2,1,0:T(8,128)(2,1)}), bf16[4,128,512]{2,1,0:T(8,128)(2,1)S(1)}, u32[]{:S(2)}, u32[]{:S(2)}) async-start(bf16[4,128,512]{2,1,0:T(8,128)(2,1)} %bitcast.8), calls=%async_computation.2 | async-start | bytes 1048576 | tf_op jit(solution)/shard_map/all_to_all | solution.py:81
  27.1 0.0 copy-done.1
  27.1 2.1 %copy.14 = bf16[2,512,512]{2,0,1:T(2,128)(2,1)} copy(bf16[2,512,512]{2,1,0:T(8,128)(2,1)S(1)} %copy-done.1) | data formatting | bytes 2097152 | tf_op args[0]
  29.2 0.8 fusion.92
  30.1 0.9 fusion.94
  30.9 0.9 fusion.96
  31.8 9.4 %all-to-all-done.2 = bf16[4,128,512]{2,1,0:T(8,128)(2,1)S(1)} async-done(((bf16[4,128,512]{2,1,0:T(8,128)(2,1)}), bf16[4,128,512]{2,1,0:T(8,128)(2,1)S(1)}, u32[]{:S(2)}, u32[]{:S(2)}) %all-to-all-start.2) | async-done | bytes 524320 | tf_op jit(solution)/shard_map/all_to_all | solution.py:81
  41.1 3.7 %all-to-all-start = ((bf16[2,512,512]{2,0,1:T(2,128)(2,1)}), bf16[2,512,512]{2,0,1:T(2,128)(2,1)S(1)}, u32[]{:S(2)}, u32[]{:S(2)}) async-start(bf16[2,512,512]{2,0,1:T(2,128)(2,1)} %copy.14), calls=%async_computation | async-start | bytes 2097152 | tf_op jit(solution)/shard_map/all_to_all | solution.py:80
  44.9 0.8 fusion.98
  45.7 0.8 fusion.100
  46.5 0.8 fusion.74
  47.4 0.8 fusion.102
  48.2 0.2 multiply_bitcast_fusion.1
  48.4 0.1 copy.25
  48.5 1.2 multiply_bitcast_fusion
  49.7 0.1 copy.26
  49.8 20.1 %all-to-all-done = bf16[2,512,512]{2,0,1:T(2,128)(2,1)S(1)} async-done(((bf16[2,512,512]{2,0,1:T(2,128)(2,1)}), bf16[2,512,512]{2,0,1:T(2,128)(2,1)S(1)}, u32[]{:S(2)}, u32[]{:S(2)}) %all-to-all-start) | async-done | bytes 1048608 | tf_op jit(solution)/shard_map/all_to_all | solution.py:80
  69.9 0.8 copy.15
  70.7 0.3 copy.27
  71.0 0.0 slice-start
  71.0 5.9 %convolution_bitcast_fusion = f32[256,2048]{1,0:T(8,128)S(1)} fusion(bf16[256,2048]{1,0:T(8,128)(2,1)S(1)} %bitcast.77, bf16[2048,2048]{1,0:T(8,128)(2,1)} %copy-done.2), kind=kOutput, calls=%fused_computation.69 | convolution fusion | flops 2147483648 | bytes 11534336 | tf_op jit(solution)/shard_map/dot_general | solution.py:60
  76.9 0.0 slice-start.1
  76.9 5.9 %convolution_bitcast_fusion.1 = f32[256,2048]{1,0:T(8,128)S(1)} fusion(bf16[256,2048]{1,0:T(8,128)(2,1)S(1)} %bitcast.78, bf16[2048,2048]{1,0:T(8,128)(2,1)} %fusion.102), kind=kOutput, calls=%fused_computation.70 | convolution fusion | flops 2147483648 | bytes 11534336 | tf_op jit(solution)/shard_map/dot_general | solution.py:60
  82.8 1.2 fusion.16
  84.0 1.1 fusion.18
  85.2 2.4 %fusion.43 = f32[256,2048]{1,0:T(8,128)S(1)} fusion(bf16[2048,2048]{1,0:T(8,128)(2,1)S(1)} %bitcast.82, bf16[128,2048]{1,0:T(8,128)(2,1)S(1)} %fusion.18, bf16[128,2048]{1,0:T(8,128)(2,1)S(1)} %get-tuple-element.8), kind=kOutput, calls=%fused_computation.147 | convolution fusion | flops 2149580800 | bytes 11534336 | tf_op jit(solution)/shard_map/dot_general | solution.py:60
  87.6 5.7 %fusion.44 = f32[256,2048]{1,0:T(8,128)S(1)} fusion(bf16[2048,2048]{1,0:T(8,128)(2,1)} %fusion.102, bf16[128,2048]{1,0:T(8,128)(2,1)S(1)} %fusion.18, bf16[128,2048]{1,0:T(8,128)(2,1)S(1)} %get-tuple-element.8), kind=kOutput, calls=%fused_computation.148 | convolution fusion | flops 2149580800 | bytes 11534336 | tf_op jit(solution)/shard_map/dot_general | solution.py:60
  93.3 1.4 %fusion.20 = (bf16[128,2048]{1,0:T(8,128)(2,1)S(1)}, bf16[128,2048]{1,0:T(8,128)(2,1)S(1)}, bf16[128,2048]{1,0:T(8,128)(2,1)S(1)}) fusion(f32[128,2048]{1,0:T(8,128)S(1)} %bitcast.71, f32[256,2048]{1,0:T(8,128)S(1)} %fusion.44, f32[256,2048]{1,0:T(8,128)S(1)} %fusion.43), kind=kLoop, calls=%fused_computation.101 | loop fusion | flops 9961472 | bytes 6815744 | tf_op jit(solution)/shard_map/convert_element_type | solution.py:92
  94.7 1.1 fusion.22
  95.9 3.4 %fusion.6 = f32[256,512]{1,0:T(8,128)S(1)} fusion(s32[512]{0:T(512)S(1)} %broadcast_add_fusion.1, s32[2048]{0:T(1024)S(1)} %broadcast_add_fusion, bf16[128,2048]{1,0:T(8,128)(2,1)S(1)} %fusion.22, bf16[128,2048]{1,0:T(8,128)(2,1)S(1)} %get-tuple-element.5), kind=kOutput, calls=%fused_computation.71 | convolution fusion | flops 562036736 | bytes 1583104 | tf_op jit(solution)/shard_map/dot_general | solution.py:60
  99.3 5.0 %fusion.8 = f32[256,512]{1,0:T(8,128)S(1)} fusion(s32[512]{0:T(512)S(1)} %broadcast_add_fusion.1, s32[2048]{0:T(1024)S(1)} %broadcast_add_fusion, bf16[128,2048]{1,0:T(8,128)(2,1)S(1)} %fusion.22, bf16[128,2048]{1,0:T(8,128)(2,1)S(1)} %get-tuple-element.5), kind=kOutput, calls=%fused_computation.72 | convolution fusion | flops 576716800 | bytes 1583104 | tf_op jit(solution)/shard_map/dot_general | solution.py:60
  104.3 0.1 fusion.106
  104.5 0.1 copy.18
  104.6 0.1 copy.19
  104.7 0.7 copy.20
  105.5 3.7 %all-to-all-start.3 = ((bf16[32,2,16,128]{3,2,1,0:T(8,128)(2,1)}), bf16[32,2,16,128]{3,2,1,0:T(8,128)(2,1)S(1)}, u32[]{:S(2)}, u32[]{:S(2)}) async-start(bf16[32,2,16,128]{3,2,1,0:T(8,128)(2,1)} %copy.20), calls=%async_computation.3 | async-start | bytes 524288 | tf_op jit(solution)/shard_map/all_to_all | solution.py:100
  109.2 0.1 fusion.109
  109.3 10.1 %all-to-all-done.3 = bf16[32,2,16,128]{3,2,1,0:T(8,128)(2,1)S(1)} async-done(((bf16[32,2,16,128]{3,2,1,0:T(8,128)(2,1)}), bf16[32,2,16,128]{3,2,1,0:T(8,128)(2,1)S(1)}, u32[]{:S(2)}, u32[]{:S(2)}) %all-to-all-start.3) | async-done | bytes 262176 | tf_op jit(solution)/shard_map/all_to_all | solution.py:100
  119.4 0.3 fusion.108
  119.8 0.3 fusion.107
  120.1 0.3 convolution_subtract_fusion
  120.5 0.4 fusion.103
  120.9 0.4 fusion.137
  121.3 0.4 fusion.135
  121.7 0.4 fusion.14
  122.0 0.1 stack.21
  122.2 0.4 fusion.13
  122.6 0.1 stack.22
  122.7 0.7 maximum_multiply_fusion
  (32 shorter events, 0.7 us)
Async XLA Ops:
  2.8 20.8 %all-to-all-start.1 = ((bf16[4,128,512]{2,1,0:T(8,128)(2,1)}), bf16[4,128,512]{2,1,0:T(8,128)(2,1)S(1)}, u32[]{:S(2)}, u32[]{:S(2)}) async-start(bf16[4,128,512]{2,1,0:T(8,128)(2,1)} %bitcast.6), calls=%async_computation.1 | async-start | bytes 1048576 | tf_op jit(solution)/shard_map/all_to_all | solution.py:81
  11.3 7.3 %copy-start.2 = (bf16[2048,2048]{1,0:T(8,128)(2,1)}, bf16[2048,2048]{1,0:T(8,128)(2,1)S(1)}, u32[]{:S(2)}) copy-start(bf16[2048,2048]{1,0:T(8,128)(2,1)S(1)} %fusion.101) | copy-start | bytes 25165828
  13.6 13.6 %copy-start.1 = (bf16[2,512,512]{2,1,0:T(8,128)(2,1)S(1)}, bf16[2,512,512]{2,1,0:T(8,128)(2,1)}, u32[]{:S(2)}) copy-start(bf16[2,512,512]{2,1,0:T(8,128)(2,1)} %param.2) | copy-start | bytes 3145732
  23.6 17.5 %all-to-all-start.2 = ((bf16[4,128,512]{2,1,0:T(8,128)(2,1)}), bf16[4,128,512]{2,1,0:T(8,128)(2,1)S(1)}, u32[]{:S(2)}, u32[]{:S(2)}) async-start(bf16[4,128,512]{2,1,0:T(8,128)(2,1)} %bitcast.8), calls=%async_computation.2 | async-start | bytes 1048576 | tf_op jit(solution)/shard_map/all_to_all | solution.py:81
  41.1 7.1 %copy-start = (bf16[4,128,512]{2,1,0:T(8,128)(2,1)}, bf16[4,128,512]{2,1,0:T(8,128)(2,1)S(1)}, u32[]{:S(2)}) copy-start(bf16[4,128,512]{2,1,0:T(8,128)(2,1)S(1)} %all-to-all-done.2) | copy-start | bytes 1572868
  41.1 28.8 %all-to-all-start = ((bf16[2,512,512]{2,0,1:T(2,128)(2,1)}), bf16[2,512,512]{2,0,1:T(2,128)(2,1)S(1)}, u32[]{:S(2)}, u32[]{:S(2)}) async-start(bf16[2,512,512]{2,0,1:T(2,128)(2,1)} %copy.14), calls=%async_computation | async-start | bytes 2097152 | tf_op jit(solution)/shard_map/all_to_all | solution.py:80
  71.0 14.2 %slice-start = ((s8[8388608]{0:T(1024)(128)(4,1)}), s8[4194304]{0:T(1024)(128)(4,1)S(1)}, s32[]{:S(2)}) async-start(s8[8388608]{0:T(1024)(128)(4,1)} %bitcast.81), calls=%async_computation.4 | async-start | bytes 8388608
  76.9 8.3 %slice-start.1 = ((s8[8388608]{0:T(1024)(128)(4,1)}), s8[4194304]{0:T(1024)(128)(4,1)S(1)}, s32[]{:S(2)}) async-start(s8[8388608]{0:T(1024)(128)(4,1)} %bitcast.81), calls=%async_computation.5 | async-start | bytes 8388608
  105.5 13.9 %all-to-all-start.3 = ((bf16[32,2,16,128]{3,2,1,0:T(8,128)(2,1)}), bf16[32,2,16,128]{3,2,1,0:T(8,128)(2,1)S(1)}, u32[]{:S(2)}, u32[]{:S(2)}) async-start(bf16[32,2,16,128]{3,2,1,0:T(8,128)(2,1)} %copy.20), calls=%async_computation.3 | async-start | bytes 524288 | tf_op jit(solution)/shard_map/all_to_all | solution.py:100
where the time goes:
time: 124 us; the launch traced here: 123 us
  waiting for transfers between devices  43.7 us (35%)
  matrix products  31.3 us (25%)
  other arithmetic  25.2 us (20%)
  starting transfers between devices  17.2 us (14%)
  local copies, waits for them, and re-layouts  5.58 us (4%)
    dot_general x6, matrix products, matmul(): return jnp.dot(left, right, preferred_element_type=jnp.float32)  28.3 us
    all_to_all x1, waiting for transfers between devices, on_device(): lax.all_to_all(near_field, 'grp', split_axis=1, concat_axis=2, tiled=True)  20.1 us
    unnamed x31, other arithmetic  14.3 us
    all_to_all x2, waiting for transfers between devices, on_device(): lax.all_to_all(part, 'grp', split_axis=0, concat_axis=1, tiled=True)  13.5 us
    all_to_all x1, waiting for transfers between devices, on_device(): lax.all_to_all(cols, ('slab', 'grp'), split_axis=0, concat_axis=0, tiled=...  10.1 us
    all_to_all x2, starting transfers between devices, on_device(): lax.all_to_all(part, 'grp', split_axis=0, concat_axis=1, tiled=True)  9.82 us
    all_to_all x1, starting transfers between devices, on_device(): lax.all_to_all(cols, ('slab', 'grp'), split_axis=0, concat_axis=0, tiled=...  3.71 us
    all_to_all x1, starting transfers between devices, on_device(): lax.all_to_all(near_field, 'grp', split_axis=1, concat_axis=2, tiled=True)  3.7 us
  transfers between devices with their start and end apart: 4, of which 4 were waited for; matrix products, arithmetic and copies ran while one was open for 16% of the time, Pallas kernels for 0%

commit v1 on v0

--- a/solution.py
+++ b/solution.py
@@ -77,7 +77,10 @@
     rows = lat_dev // group_count
     angles = AV // devices
     coded = [jnp.exp2(lens_phase[k] * PHASE_CODE).astype(jnp.bfloat16) for k in range(steps)]
-    field = lax.all_to_all(near_field, "grp", split_axis=1, concat_axis=2, tiled=True)
+    field = jnp.concatenate(
+        lax.all_to_all(jnp.stack(jnp.split(near_field, lax.axis_size("grp"), axis=1)), "grp", 0, 0),
+        axis=2,
+    )
     coded = [lax.all_to_all(part, "grp", split_axis=0, concat_axis=1, tiled=True) for part in coded]
     prop_cos, prop_sin = propagator(points)
     both = field.reshape(2 * rows, points)

time: 124 us -> 117 us (0.944)
  matrix products: 31.3 us -> 24.5 us
  other arithmetic: 25.2 us -> 19.3 us
  local copies, waits for them, and re-layouts: 5.58 us -> 9.2 us
  waiting for transfers between devices: 43.7 us -> 45.9 us
    unnamed x31 -> x32, other arithmetic: 14.3 us -> 7.27 us
    dot_general x6, matrix products: 28.3 us -> 21.5 us  [matmul(): return jnp.dot(left, right, preferred_element_type=jnp.float32)]
    unnamed x14 -> x19, local copies, waits for them, and re-layouts: 3.35 us -> 6.86 us
    all_to_all x2, waiting for transfers between devices: 13.5 us -> 15.6 us  [on_device(): lax.all_to_all(part, 'grp', split_axis=0, concat_axis=1, tiled=True)]
  transfers between devices with their start and end apart: 4 -> 4, of which waited for: 4 -> 4; matrix products, arithmetic and copies ran while one was open for 16% -> 10% of each run, Pallas kernels for 0% -> 0%
where the time goes in v1:
time: 117 us
  waiting for transfers between devices  45.9 us (39%)
  matrix products  24.5 us (21%)
  other arithmetic  19.3 us (16%)
  starting transfers between devices  17.2 us (15%)
  local copies, waits for them, and re-layouts  9.2 us (8%)
    dot_general x6, matrix products, matmul(): return jnp.dot(left, right, preferred_element_type=jnp.float32)  21.5 us
    all_to_all x1, waiting for transfers between devices, on_device(): lax.all_to_all(jnp.stack(jnp.split(near_field, lax.axis_size('grp'), axis...  20.1 us
    all_to_all x2, waiting for transfers between devices, on_device(): lax.all_to_all(part, 'grp', split_axis=0, concat_axis=1, tiled=True)  15.6 us
    all_to_all x1, waiting for transfers between devices, on_device(): lax.all_to_all(cols, ('slab', 'grp'), split_axis=0, concat_axis=0, tiled=...  10.1 us
    all_to_all x2, starting transfers between devices, on_device(): lax.all_to_all(part, 'grp', split_axis=0, concat_axis=1, tiled=True)  9.82 us
    unnamed x32, other arithmetic  7.27 us
    unnamed x19, local copies, waits for them, and re-layouts  6.86 us
    all_to_all x1, starting transfers between devices, on_device(): lax.all_to_all(cols, ('slab', 'grp'), split_axis=0, concat_axis=0, tiled=...  3.71 us
  transfers between devices with their start and end apart: 4, of which 4 were waited for; matrix products, arithmetic and copies ran while one was open for 10% of the time, Pallas kernels for 0%

profile of v1, /device:TPU:0, one launch (start us, length us, event | category | flops | bytes accessed | tf_op | source)
XLA Modules:
  0.0 116.6 jit_solution(632398541088401806)
XLA Ops:
  0.0 2.8 %exponential_convert_fusion.1 = (bf16[1,512,512]{2,1,0:T(8,128)(2,1)}, bf16[1,512,512]{2,1,0:T(8,128)(2,1)}) fusion(f32[2,512,512]{2,1,0:T(8,128)} %param.3), kind=kLoop, calls=%fused_computation.137 | loop fusion | flops 1048576 | bytes 3145728 | tf_op jit(solution)/shard_map/convert_element_type | solution.py:79
  2.8 6.3 %all-to-all-start.1 = ((bf16[4,128,512]{2,1,0:T(8,128)(2,1)}), bf16[4,128,512]{2,1,0:T(8,128)(2,1)S(1)}, u32[]{:S(2)}, u32[]{:S(2)}) async-start(bf16[4,128,512]{2,1,0:T(8,128)(2,1)} %bitcast.7), calls=%async_computation.1 | async-start | bytes 1048576 | tf_op jit(solution)/shard_map/all_to_all | solution.py:84
  9.2 1.4 %fusion.27 = (bf16[128,2048]{1,0:T(8,128)(2,1)S(1)}, bf16[128,2048]{1,0:T(8,128)(2,1)S(1)}) fusion(s32[128]{0:T(128)S(1)} %iota.18, s32[2048]{0:T(1024)S(1)} %iota.21), kind=kLoop, calls=%fused_computation.106 | loop fusion | flops 10223616 | bytes 1057280 | tf_op jit(solution)/shard_map/convert_element_type | solution.py:47
  11.3 0.0 copy-start.2
  11.3 3.3 %copy-done.2 = bf16[2048,2048]{1,0:T(8,128)(2,1)} copy-done((bf16[2048,2048]{1,0:T(8,128)(2,1)}, bf16[2048,2048]{1,0:T(8,128)(2,1)S(1)}, u32[]{:S(2)}) %copy-start.2) | copy-done | bytes 8388632
  14.6 0.0 copy-start.1
  15.0 0.0 copy-start.3
  15.0 3.2 %copy-done.3 = bf16[2048,2048]{1,0:T(8,128)(2,1)} copy-done((bf16[2048,2048]{1,0:T(8,128)(2,1)}, bf16[2048,2048]{1,0:T(8,128)(2,1)S(1)}, u32[]{:S(2)}) %copy-start.3) | copy-done | bytes 8388632
  18.2 0.0 copy-done.1
  18.2 0.1 slice_bitcast_fusion.3
  18.3 5.3 %all-to-all-done.1 = bf16[4,128,512]{2,1,0:T(8,128)(2,1)S(1)} async-done(((bf16[4,128,512]{2,1,0:T(8,128)(2,1)}), bf16[4,128,512]{2,1,0:T(8,128)(2,1)S(1)}, u32[]{:S(2)}, u32[]{:S(2)}) %all-to-all-start.1) | async-done | bytes 524320 | tf_op jit(solution)/shard_map/all_to_all | solution.py:84
  23.6 3.5 %all-to-all-start.2 = ((bf16[4,128,512]{2,1,0:T(8,128)(2,1)}), bf16[4,128,512]{2,1,0:T(8,128)(2,1)S(1)}, u32[]{:S(2)}, u32[]{:S(2)}) async-start(bf16[4,128,512]{2,1,0:T(8,128)(2,1)} %bitcast.9), calls=%async_computation.2 | async-start | bytes 1048576 | tf_op jit(solution)/shard_map/all_to_all | solution.py:84
  27.1 1.1 pad_maximum_fusion
  28.2 0.8 fusion.92
  29.1 0.8 fusion.94
  29.9 0.9 fusion.96
  30.8 10.3 %all-to-all-done.2 = bf16[4,128,512]{2,1,0:T(8,128)(2,1)S(1)} async-done(((bf16[4,128,512]{2,1,0:T(8,128)(2,1)}), bf16[4,128,512]{2,1,0:T(8,128)(2,1)S(1)}, u32[]{:S(2)}, u32[]{:S(2)}) %all-to-all-start.2) | async-done | bytes 524320 | tf_op jit(solution)/shard_map/all_to_all | solution.py:84
  41.1 3.7 %all-to-all-start = ((bf16[4,2,128,512]{3,2,1,0:T(8,128)(2,1)}), bf16[4,2,128,512]{3,2,1,0:T(8,128)(2,1)S(1)}, u32[]{:S(2)}, u32[]{:S(2)}) async-start(bf16[4,2,128,512]{3,2,1,0:T(8,128)(2,1)} %pad_maximum_fusion), calls=%async_computation | async-start | bytes 2097152 | tf_op jit(solution)/shard_map/all_to_all | solution.py:81
  44.9 0.8 fusion.98
  45.7 0.8 fusion.100
  46.5 0.8 fusion.74
  47.4 0.8 fusion.102
  48.2 0.0 copy-done
  48.2 0.2 multiply_bitcast_fusion.1
  48.4 0.1 copy.24
  48.5 1.2 %multiply_bitcast_fusion = f32[4,16,8,512]{3,2,1,0:T(8,128)S(1)} fusion(bf16[4,128,512]{2,1,0:T(8,128)(2,1)} %copy-done), kind=kLoop, calls=%fused_computation.127 | loop fusion | flops 524288 | bytes 1572864
  49.7 0.1 copy.25
  49.8 20.1 %all-to-all-done = bf16[4,2,128,512]{3,2,1,0:T(8,128)(2,1)S(1)} async-done(((bf16[4,2,128,512]{3,2,1,0:T(8,128)(2,1)}), bf16[4,2,128,512]{3,2,1,0:T(8,128)(2,1)S(1)}, u32[]{:S(2)}, u32[]{:S(2)}) %all-to-all-start) | async-done | bytes 1048608 | tf_op jit(solution)/shard_map/all_to_all | solution.py:81
  69.9 0.8 copy.14
  70.7 0.0 slice-start.2
  70.7 0.3 copy.26
  71.0 0.0 slice-start.3
  71.0 0.0 slice-start
  71.0 5.9 %fusion.293 = f32[256,2048]{1,0:T(8,128)S(1)} fusion(bf16[256,2048]{1,0:T(8,128)(2,1)S(1)} %bitcast.80, bf16[2048,2048]{1,0:T(8,128)(2,1)} %copy-done.2), kind=kOutput, calls=%fused_computation.423 | convolution fusion | flops 2147483648 | bytes 11534336 | tf_op jit(solution)/shard_map/dot_general | solution.py:60
  76.9 0.0 slice-done.2
  76.9 0.0 slice-done.3
  77.0 0.0 slice-start.1
  77.0 2.4 %fusion.292 = f32[256,2048]{1,0:T(8,128)S(1)} fusion(bf16[256,2048]{1,0:T(8,128)(2,1)S(1)} %bitcast.81, bf16[2048,2048]{1,0:T(8,128)(2,1)S(1)} %bitcast.87), kind=kOutput, calls=%fused_computation.422 | convolution fusion | flops 2147483648 | bytes 11534336 | tf_op jit(solution)/shard_map/dot_general | solution.py:60
  79.4 1.2 %fusion.16 = (bf16[128,2048]{1,0:T(8,128)(2,1)S(1)}, bf16[128,2048]{1,0:T(8,128)(2,1)S(1)}, bf16[128,2048]{1,0:T(8,128)(2,1)S(1)}) fusion(f32[128,2048]{1,0:T(8,128)S(1)} %bitcast.76, f32[256,2048]{1,0:T(8,128)S(1)} %fusion.292, f32[256,2048]{1,0:T(8,128)S(1)} %fusion.293), kind=kLoop, calls=%fused_computation.95 | loop fusion | flops 9961472 | bytes 6815744 | tf_op jit(solution)/shard_map/convert_element_type | solution.py:95
  80.6 1.1 fusion.18
  81.7 2.4 %fusion.43 = f32[256,2048]{1,0:T(8,128)S(1)} fusion(bf16[2048,2048]{1,0:T(8,128)(2,1)S(1)} %bitcast.85, bf16[128,2048]{1,0:T(8,128)(2,1)S(1)} %fusion.18, bf16[128,2048]{1,0:T(8,128)(2,1)S(1)} %get-tuple-element.8), kind=kOutput, calls=%fused_computation.146 | convolution fusion | flops 2149580800 | bytes 11534336 | tf_op jit(solution)/shard_map/dot_general | solution.py:60
  84.1 2.4 %fusion.44 = f32[256,2048]{1,0:T(8,128)S(1)} fusion(bf16[2048,2048]{1,0:T(8,128)(2,1)S(1)} %bitcast.87, bf16[128,2048]{1,0:T(8,128)(2,1)S(1)} %fusion.18, bf16[128,2048]{1,0:T(8,128)(2,1)S(1)} %get-tuple-element.8), kind=kOutput, calls=%fused_computation.147 | convolution fusion | flops 2149580800 | bytes 11534336 | tf_op jit(solution)/shard_map/dot_general | solution.py:60
  86.5 1.4 %fusion.20 = (bf16[128,2048]{1,0:T(8,128)(2,1)S(1)}, bf16[128,2048]{1,0:T(8,128)(2,1)S(1)}, bf16[128,2048]{1,0:T(8,128)(2,1)S(1)}) fusion(f32[128,2048]{1,0:T(8,128)S(1)} %bitcast.74, f32[256,2048]{1,0:T(8,128)S(1)} %fusion.44, f32[256,2048]{1,0:T(8,128)S(1)} %fusion.43), kind=kLoop, calls=%fused_computation.99 | loop fusion | flops 9961472 | bytes 6815744 | tf_op jit(solution)/shard_map/convert_element_type | solution.py:95
  88.0 1.1 fusion.22
  89.1 3.4 %fusion.6 = f32[256,512]{1,0:T(8,128)S(1)} fusion(s32[512]{0:T(512)S(1)} %broadcast_add_fusion.1, s32[2048]{0:T(1024)S(1)} %broadcast_add_fusion, bf16[128,2048]{1,0:T(8,128)(2,1)S(1)} %fusion.22, bf16[128,2048]{1,0:T(8,128)(2,1)S(1)} %get-tuple-element.5), kind=kOutput, calls=%fused_computation.69 | convolution fusion | flops 562036736 | bytes 1583104 | tf_op jit(solution)/shard_map/dot_general | solution.py:60
  92.5 5.0 %fusion.8 = f32[256,512]{1,0:T(8,128)S(1)} fusion(s32[512]{0:T(512)S(1)} %broadcast_add_fusion.1, s32[2048]{0:T(1024)S(1)} %broadcast_add_fusion, bf16[128,2048]{1,0:T(8,128)(2,1)S(1)} %fusion.22, bf16[128,2048]{1,0:T(8,128)(2,1)S(1)} %get-tuple-element.5), kind=kOutput, calls=%fused_computation.70 | convolution fusion | flops 576716800 | bytes 1583104 | tf_op jit(solution)/shard_map/dot_general | solution.py:60
  97.5 0.1 fusion.106
  97.7 0.1 copy.17
  97.8 0.1 copy.18
  98.0 0.7 copy.19
  98.7 3.7 %all-to-all-start.3 = ((bf16[32,2,16,128]{3,2,1,0:T(8,128)(2,1)}), bf16[32,2,16,128]{3,2,1,0:T(8,128)(2,1)S(1)}, u32[]{:S(2)}, u32[]{:S(2)}) async-start(bf16[32,2,16,128]{3,2,1,0:T(8,128)(2,1)} %copy.19), calls=%async_computation.3 | async-start | bytes 524288 | tf_op jit(solution)/shard_map/all_to_all | solution.py:103
  102.4 0.1 fusion.109
  102.5 10.1 %all-to-all-done.3 = bf16[32,2,16,128]{3,2,1,0:T(8,128)(2,1)S(1)} async-done(((bf16[32,2,16,128]{3,2,1,0:T(8,128)(2,1)}), bf16[32,2,16,128]{3,2,1,0:T(8,128)(2,1)S(1)}, u32[]{:S(2)}, u32[]{:S(2)}) %all-to-all-start.3) | async-done | bytes 262176 | tf_op jit(solution)/shard_map/all_to_all | solution.py:103
  112.6 0.3 fusion.108
  113.0 0.3 fusion.107
  113.3 0.3 convolution_subtract_fusion
  113.7 0.4 fusion.103
  114.1 0.4 fusion.137
  114.5 0.4 fusion.135
  114.9 0.4 fusion.14
  115.3 0.1 stack.41
  115.4 0.4 fusion.13
  115.8 0.1 stack.42
  115.9 0.7 maximum_multiply_fusion
  (40 shorter events, 1.0 us)
Async XLA Ops:
  2.8 20.8 %all-to-all-start.1 = ((bf16[4,128,512]{2,1,0:T(8,128)(2,1)}), bf16[4,128,512]{2,1,0:T(8,128)(2,1)S(1)}, u32[]{:S(2)}, u32[]{:S(2)}) async-start(bf16[4,128,512]{2,1,0:T(8,128)(2,1)} %bitcast.7), calls=%async_computation.1 | async-start | bytes 1048576 | tf_op jit(solution)/shard_map/all_to_all | solution.py:84
  11.3 3.3 %copy-start.2 = (bf16[2048,2048]{1,0:T(8,128)(2,1)}, bf16[2048,2048]{1,0:T(8,128)(2,1)S(1)}, u32[]{:S(2)}) copy-start(bf16[2048,2048]{1,0:T(8,128)(2,1)S(1)} %fusion.101) | copy-start | bytes 25165828
  14.6 3.6 %copy-start.1 = (bf16[2,512,512]{2,1,0:T(8,128)(2,1)S(1)}, bf16[2,512,512]{2,1,0:T(8,128)(2,1)}, u32[]{:S(2)}) copy-start(bf16[2,512,512]{2,1,0:T(8,128)(2,1)} %param.2) | copy-start | bytes 3145732
  15.0 3.2 %copy-start.3 = (bf16[2048,2048]{1,0:T(8,128)(2,1)}, bf16[2048,2048]{1,0:T(8,128)(2,1)S(1)}, u32[]{:S(2)}) copy-start(bf16[2048,2048]{1,0:T(8,128)(2,1)S(1)} %fusion.90) | copy-start | bytes 25165828
  23.6 17.5 %all-to-all-start.2 = ((bf16[4,128,512]{2,1,0:T(8,128)(2,1)}), bf16[4,128,512]{2,1,0:T(8,128)(2,1)S(1)}, u32[]{:S(2)}, u32[]{:S(2)}) async-start(bf16[4,128,512]{2,1,0:T(8,128)(2,1)} %bitcast.9), calls=%async_computation.2 | async-start | bytes 1048576 | tf_op jit(solution)/shard_map/all_to_all | solution.py:84
  41.1 7.1 %copy-start = (bf16[4,128,512]{2,1,0:T(8,128)(2,1)}, bf16[4,128,512]{2,1,0:T(8,128)(2,1)S(1)}, u32[]{:S(2)}) copy-start(bf16[4,128,512]{2,1,0:T(8,128)(2,1)S(1)} %all-to-all-done.2) | copy-start | bytes 1572868
  41.1 28.8 %all-to-all-start = ((bf16[4,2,128,512]{3,2,1,0:T(8,128)(2,1)}), bf16[4,2,128,512]{3,2,1,0:T(8,128)(2,1)S(1)}, u32[]{:S(2)}, u32[]{:S(2)}) async-start(bf16[4,2,128,512]{3,2,1,0:T(8,128)(2,1)} %pad_maximum_fusion), calls=%async_computation | async-start | bytes 2097152 | tf_op jit(solution)/shard_map/all_to_all | solution.py:81
  70.7 6.2 %slice-start.2 = ((s8[8388608]{0:T(1024)(128)(4,1)}), s8[4194304]{0:T(1024)(128)(4,1)S(1)}, s32[]{:S(2)}) async-start(s8[8388608]{0:T(1024)(128)(4,1)} %bitcast.86), calls=%async_computation.6 | async-start | bytes 8388608
  71.0 5.9 %slice-start.3 = ((s8[8388608]{0:T(1024)(128)(4,1)}), s8[4194304]{0:T(1024)(128)(4,1)S(1)}, s32[]{:S(2)}) async-start(s8[8388608]{0:T(1024)(128)(4,1)} %bitcast.86), calls=%async_computation.7 | async-start | bytes 8388608
  71.0 10.7 %slice-start = ((s8[8388608]{0:T(1024)(128)(4,1)}), s8[4194304]{0:T(1024)(128)(4,1)S(1)}, s32[]{:S(2)}) async-start(s8[8388608]{0:T(1024)(128)(4,1)} %bitcast.84), calls=%async_computation.4 | async-start | bytes 8388608
  77.0 4.8 %slice-start.1 = ((s8[8388608]{0:T(1024)(128)(4,1)}), s8[4194304]{0:T(1024)(128)(4,1)S(1)}, s32[]{:S(2)}) async-start(s8[8388608]{0:T(1024)(128)(4,1)} %bitcast.84), calls=%async_computation.5 | async-start | bytes 8388608
  98.7 13.9 %all-to-all-start.3 = ((bf16[32,2,16,128]{3,2,1,0:T(8,128)(2,1)}), bf16[32,2,16,128]{3,2,1,0:T(8,128)(2,1)S(1)}, u32[]{:S(2)}, u32[]{:S(2)}) async-start(bf16[32,2,16,128]{3,2,1,0:T(8,128)(2,1)} %copy.19), calls=%async_computation.3 | async-start | bytes 524288 | tf_op jit(solution)/shard_map/all_to_all | solution.py:103
